TPU v7x, 32 devices: a whole 2x2x4 slice. The times are simulated.
32 devices in a mesh: groups: 2 (over x), ctx: 16 (over z, y, core).
Axes of the slice: x: 2, y: 2, z: 4, core: 2. Of those that a mesh axis runs over, the one named last changes fastest.
Arguments:
- queries: bfloat16 [2048, 4096], P(('groups', 'ctx')), parts along dimension 0, may hold values from -256 to 256
- text_keys: bfloat16 [2048, 512], P(('groups', 'ctx')), parts along dimension 0, may hold values from -4 to 4
- text_values: bfloat16 [2048, 512], P(('groups', 'ctx')), parts along dimension 0, may hold values from -5 to 5
- image_features: bfloat16 [16384, 256], P(('groups', 'ctx')), parts along dimension 0, may hold values from -300 to 300
- kv_weight: bfloat16 [8192, 1024], P('ctx'), may hold values from -0.0625 to 0.0625
- image_grids: int32 [32, 3], P(('groups', 'ctx')), parts along dimension 0, may hold values from 0 to 58, as said below
Outputs:
- attention: bfloat16 [2048, 4096], P(('groups', 'ctx')), parts along dimension 0
- cache_keys: bfloat16 [2048, 512], P(('groups', 'ctx')), parts along dimension 0
- cache_values: bfloat16 [2048, 512], P(('groups', 'ctx')), parts along dimension 0
There are 2 independent parts, one for each index of `groups`. A program takes and returns all parts, laid end to end along the dimension named above; an argument that names none is the same for every part. Nothing has to cross between parts.
Inputs may be any that keep to these rules, and one draw needn't show every extreme that they name: `image_grids`: row b describes the one image of context shard b: offset o, grid rows gh and grid columns gw with 2 <= gh, gw <= 4; its tokens take positions b * 64 + o to b * 64 + o + gh * gw - 1, token k at grid row k // gw and column k % gw; o + gh * gw <= 62; some shard has a 4 x 4 image.
All inputs are finite; a program needn't handle non-finite values.
Results may differ from a plain program's by a relative error of at most 0.0053.
Values may be sent and summed in bfloat16 or wider, within the bound.
No kernel may reach another device: no remote copies, remote signals or barrier semaphores. Data moves between devices by JAX's collectives and lax.ppermute only.
A program may use at most 128 MiB of HBM per device.

v0:
```python
import math
import jax
import jax.numpy as jnp
from jax import lax
from jax.sharding import PartitionSpec as P

D = 8192
HEAD_DIM = 128
GRID = 4


def rope_tables(time_ids, height_ids, width_ids):
    half_dim = HEAD_DIM // 2
    first_bound = HEAD_DIM // 8
    second_bound = first_bound + 3 * HEAD_DIM // 16
    pair_index = jnp.arange(half_dim, dtype=jnp.int32)
    inv_freq = 1000000.0 ** (-(2.0 * pair_index.astype(jnp.float32)) / HEAD_DIM)
    chosen = jnp.where(
        pair_index[None, :] < first_bound,
        time_ids[:, None],
        jnp.where(pair_index[None, :] < second_bound, height_ids[:, None], width_ids[:, None]),
    )
    angles = chosen.astype(jnp.float32) * inv_freq[None, :]
    cosine = jnp.concatenate([jnp.cos(angles), jnp.cos(angles)], axis=1)
    sine_table = jnp.concatenate([jnp.sin(angles), jnp.sin(angles)], axis=1)
    return (cosine, sine_table)


def rotate(key_heads, cosine, sine_table):
    half_dim = HEAD_DIM // 2
    turned = jnp.concatenate([-key_heads[..., half_dim:], key_heads[..., :half_dim]], axis=-1)
    return key_heads * cosine[:, None, :] + turned * sine_table[:, None, :]


def prepare(query_rows, kv_count, head_group):
    count_rows = query_rows.shape[0]
    shaped = query_rows.reshape(count_rows, kv_count, head_group, HEAD_DIM)
    return shaped.transpose(1, 2, 0, 3).reshape(kv_count, head_group * count_rows, HEAD_DIM)


def finish(summed, totals, count_rows, kv_count, head_group):
    blended = summed / totals[..., None]
    blended = blended.reshape(kv_count, head_group, count_rows, HEAD_DIM).transpose(2, 0, 1, 3)
    return blended.reshape(count_rows, kv_count * head_group * HEAD_DIM).astype(jnp.bfloat16)


def update(carry_state, query_set, positions, block_keys, block_values, key_start):
    running_max, running_sum, running_out = carry_state
    score_scale = 1.0 / math.sqrt(HEAD_DIM)
    scores = (
        jnp.einsum("grd,kgd->grk", query_set, block_keys, preferred_element_type=jnp.float32)
        * score_scale
    )
    key_pos = key_start + jnp.arange(block_keys.shape[0], dtype=jnp.int32)
    allowed = key_pos[None, None, :] <= positions[None, :, None]
    scores = jnp.where(allowed, scores, -1e30)
    new_max = jnp.maximum(running_max, jnp.max(scores, axis=-1))
    shrink = jnp.exp(running_max - new_max)
    weight = jnp.where(allowed, jnp.exp(scores - new_max[..., None]), 0.0)
    running_sum = running_sum * shrink + jnp.sum(weight, axis=-1)
    running_out = running_out * shrink[..., None] + jnp.einsum(
        "grk,kgd->grd",
        weight.astype(jnp.bfloat16),
        block_values,
        preferred_element_type=jnp.float32,
    )
    return (new_max, running_sum, running_out)


def body(queries, text_keys, text_values, image_features, kv_weight, image_grids):
    ctx_index = lax.axis_index("ctx")
    row_count = queries.shape[0]
    kv_width = text_keys.shape[1]
    kv_count = kv_width // HEAD_DIM
    head_group = queries.shape[1] // kv_width
    slot_count = GRID * GRID
    partial_kv = lax.dot_general(
        image_features, kv_weight, (((0,), (0,)), ((), ())), preferred_element_type=jnp.float32
    )
    feature_f32 = image_features.astype(jnp.float32)
    square_sums = jnp.sum(feature_f32 * feature_f32, axis=0)
    raw_kv, power_total = (
        lax.psum_scatter(partial_kv, "ctx", scatter_dimension=0, tiled=True),
        lax.psum_scatter(square_sums, "ctx", scatter_dimension=0, tiled=True),
    )
    normed = raw_kv * lax.rsqrt(power_total / D + 1e-06)[:, None]
    offset = image_grids[0, 0]
    grid_tall = image_grids[0, 1]
    grid_wide = image_grids[0, 2]
    within = jnp.arange(slot_count, dtype=jnp.int32)
    image_start = ctx_index * row_count + offset
    time_ids = jnp.broadcast_to(image_start, (slot_count,))
    height_ids = image_start + within // grid_wide
    width_ids = image_start + within % grid_wide
    cosine, sine_table = rope_tables(time_ids, height_ids, width_ids)
    key_heads = normed[:, :kv_width].reshape(slot_count, kv_count, HEAD_DIM)
    image_keys = (
        rotate(key_heads, cosine, sine_table).reshape(slot_count, kv_width).astype(jnp.bfloat16)
    )
    image_values = normed[:, kv_width:].astype(jnp.bfloat16)
    live_slot = within < grid_tall * grid_wide
    local_rows = jnp.arange(row_count, dtype=jnp.int32)
    one_hot = ((local_rows[:, None] == offset + within[None, :]) & live_slot[None, :]).astype(
        jnp.bfloat16
    )
    image_rows = (local_rows >= offset) & (local_rows < offset + grid_tall * grid_wide)
    placed = jnp.dot(
        one_hot,
        jnp.concatenate([image_keys, image_values], axis=1),
        preferred_element_type=jnp.float32,
    ).astype(jnp.bfloat16)
    cache_keys = jnp.where(image_rows[:, None], placed[:, :kv_width], text_keys)
    cache_values = jnp.where(image_rows[:, None], placed[:, kv_width:], text_values)
    half_rows = row_count // 2
    lead_queries = queries[:half_rows]
    trail_queries = queries[half_rows:]
    trail_base = ctx_index * row_count + half_rows
    lead_base = ctx_index * row_count
    query_sets = jnp.stack(
        [prepare(lead_queries, kv_count, head_group), prepare(trail_queries, kv_count, head_group)]
    )
    query_span = head_group * half_rows
    row_pos = jnp.arange(query_span, dtype=jnp.int32) % half_rows
    base_rows = jnp.stack([lead_base, trail_base])
    query_pos = base_rows[:, None] + row_pos[None, :]
    limits = base_rows + half_rows - 1
    initial = (
        jnp.full((2, kv_count, query_span), -1e30, jnp.float32),
        jnp.zeros((2, kv_count, query_span), jnp.float32),
        jnp.zeros((2, kv_count, query_span, HEAD_DIM), jnp.float32),
    )
    piece_keys = lax.all_gather(cache_keys, "ctx", axis=0, tiled=True)
    piece_values = lax.all_gather(cache_values, "ctx", axis=0, tiled=True)
    piece_size = piece_keys.shape[0]
    block_size = math.gcd(piece_size, 512)
    block_count = piece_size // block_size
    split_keys = piece_keys.reshape(block_count, block_size, kv_count, HEAD_DIM)
    split_values = piece_values.reshape(block_count, block_size, kv_count, HEAD_DIM)

    def scan_step(carried_state, scan_item):
        block_keys, block_values, number = scan_item
        key_start = number * block_size
        outcome = []
        for half_index in range(2):
            half_state = tuple((member[half_index] for member in carried_state))
            updated = lax.cond(
                key_start <= limits[half_index],
                lambda current: update(
                    current,
                    query_sets[half_index],
                    query_pos[half_index],
                    block_keys,
                    block_values,
                    key_start,
                ),
                lambda current: current,
                half_state,
            )
            outcome.append(updated)
        stacked = tuple(
            (
                jnp.stack([outcome[0][number_index], outcome[1][number_index]])
                for number_index in range(3)
            )
        )
        return (stacked, None)

    result_state, unused_out = lax.scan(
        scan_step, initial, (split_keys, split_values, jnp.arange(block_count, dtype=jnp.int32))
    )
    running_max, running_sum, running_out = result_state
    lead_out = finish(running_out[0], running_sum[0], half_rows, kv_count, head_group)
    trail_out = finish(running_out[1], running_sum[1], half_rows, kv_count, head_group)
    attention = jnp.concatenate([lead_out, trail_out], axis=0)
    return (attention, cache_keys, cache_values)


def solution(mesh):
    in_specs = (
        P(("groups", "ctx"), None),
        P(("groups", "ctx"), None),
        P(("groups", "ctx"), None),
        P(("groups", "ctx"), None),
        P("ctx", None),
        P(("groups", "ctx"), None),
    )
    out_specs = (P(("groups", "ctx"), None), P(("groups", "ctx"), None), P(("groups", "ctx"), None))
    return jax.shard_map(body, mesh=mesh, in_specs=in_specs, out_specs=out_specs, check_vma=False)
```

profile of v0, /device:TPU:25, one launch (start us, length us, event | category | flops | bytes accessed | tf_op | source)
XLA Modules:
  0.0 195.3 jit_solution(3191314341069254623)
XLA Ops:
  7.3 1.1 copy-done
  8.4 2.4 %fusion.47 = f32[256,1024]{1,0:T(8,128)} fusion(bf16[512,256]{1,0:T(8,128)(2,1)} %param.15, bf16[512,1024]{1,0:T(8,128)(2,1)S(1)} %copy-done), kind=kOutput, calls=%fused_computation.104 | convolution fusion | flops 268435456 | bytes 2359296 | tf_op jit(solution)/shard_map/dot_general | solution.py:77
  10.9 0.6 fusion.46
  16.1 0.6 dynamic-slice
  17.4 25.9 %all-reduce = f32[256]{0:T(256)S(1)} all-reduce(f32[256]{0:T(256)S(1)} %multiply_reduce_fusion), channel_id=3, replica_groups=mesh['groups'=2,'ctx'=16] {'ctx'}, use_global_device_ids=true, to_apply=%region_2.0.clone | all-reduce | flops 256 | bytes 2048
  43.3 0.7 iota_add_fusion.2
  44.0 0.7 compare_and_fusion
  44.7 0.8 fusion.39
  45.8 21.6 %reduce-scatter.2.cloned.1.call-done = f32[16,1024]{1,0:T(8,128)} async-done(((f32[256,1024]{1,0:T(8,128)}), f32[16,1024]{1,0:T(8,128)}) %reduce-scatter.2.cloned.1.call-update) | async-done | bytes 65552 | tf_op jit(solution)/shard_map/reduce_scatter | solution.py:83
  67.4 0.9 broadcast_multiply_fusion
  68.5 0.2 convolution_convert_fusion
  68.7 0.7 slice_select_fusion
  69.5 0.7 all-gather.5.cloned.1.call-update
  70.5 0.8 copy.26
  71.4 37.9 %all-gather.3.cloned.1.call-done = bf16[1024,512]{1,0:T(8,128)(2,1)} async-done(((bf16[64,512]{1,0:T(8,128)(2,1)}), bf16[1024,512]{1,0:T(8,128)(2,1)}) %all-gather.3.cloned.1.call-update) | async-done | bytes 1048592 | tf_op jit(solution)/shard_map/all_gather | solution.py:132
  109.3 2.2 %reshape.193 = bf16[2,512,4,128]{3,2,1,0:T(4,128)(2,1)} reshape(bf16[1024,512]{1,0:T(8,128)(2,1)} %all-gather.3.cloned.1.call-done) | data formatting | bytes 2097152 | tf_op jit(solution)/shard_map/reshape | solution.py:137
  111.4 37.4 %all-gather.5.cloned.1.call-done = bf16[1024,512]{1,0:T(8,128)(2,1)} async-done(((bf16[64,512]{1,0:T(8,128)(2,1)}), bf16[1024,512]{1,0:T(8,128)(2,1)}) %all-gather.5.cloned.1.call-update) | async-done | bytes 1048592 | tf_op jit(solution)/shard_map/all_gather | solution.py:133
  148.9 2.1 %reshape.194 = bf16[2,512,4,128]{3,2,1,0:T(4,128)(2,1)} reshape(bf16[1024,512]{1,0:T(8,128)(2,1)} %all-gather.5.cloned.1.call-done) | data formatting | bytes 2097152 | tf_op jit(solution)/shard_map/reshape | solution.py:138
  151.1 35.4 %while.15 = (s32[]{:T(128)}, f32[2,4,256]{2,1,0:T(4,128)S(1)}, f32[2,4,256]{2,1,0:T(4,128)S(1)}, f32[2,4,256,128]{3,2,1,0:T(8,128)S(1)}, s32[2]{0:T(128)S(1)}, /...) while((s32[]{:T(128)}, f32[2,4,256]{2,1,0:T(4,128)S(1)}, ...), condition=%wide.region_12.13_spmd.clone, body=%wide.region_3.12_spmd.clone.sunk | while | flops 551560704 | bytes 36390424 | solution.py:168
  151.1 0.7 dynamic_slice.19
  152.5 0.6 fusion.57
  153.8 0.6 slice_bitcast_fusion.10
  154.5 0.5 copy-done.1
  155.0 0.3 copy-done.2
  155.3 0.4 constant_dynamic-slice_fusion.3
  155.7 0.7 copy.87
  156.5 5.1 %conditional.6 = (f32[1,4,256]{2,1,0:T(4,128)}, f32[1,4,256]{2,1,0:T(4,128)S(1)}, f32[1,4,256,128]{3,2,1,0:T(8,128)S(1)}) conditional(s32[]{:T(128)} %convert_element_type.81, (f32[4,256]{1,0:T(4,128)}, f32[4,256]{1,0:T(4,128)S(1)}, f32[4,256,128]{2,1,0:T(8,128)S(1)}) %tuple.139, (s32[]{:T(128)}, s32[2,256]{1,0:T(2,128)S(1)}, ...), branch_computations={%region_8.8_spmd, %region_9.11_spmd} | conditional | flops 275646976 | bytes 9239580 | solution.py:146
  156.7 0.6 fusion.14
  157.3 0.6 max.5
  157.8 1.5 fusion.16
  159.3 0.7 add_bitcast_fusion.1
  160.0 1.6 fusion.17
  162.3 0.7 copy.93
  162.9 5.1 %conditional.7 = (f32[1,4,256]{2,1,0:T(4,128)}, f32[1,4,256]{2,1,0:T(4,128)S(1)}, f32[1,4,256,128]{3,2,1,0:T(8,128)S(1)}) conditional(s32[]{:T(128)} %convert_element_type.82, (f32[4,256]{1,0:T(4,128)}, f32[4,256]{1,0:T(4,128)S(1)}, f32[4,256,128]{2,1,0:T(8,128)S(1)}) %tuple.141, (s32[]{:T(128)}, s32[2,256]{1,0:T(2,128)S(1)}, ...), branch_computations={%region_4.4_spmd, %region_5.7_spmd} | conditional | flops 275646976 | bytes 9239580 | solution.py:146
  163.1 0.6 fusion.2
  163.7 0.6 max.4
  164.3 1.5 fusion.4
  165.7 0.7 add_bitcast_fusion
  166.4 1.6 fusion.5
  168.0 0.7 pad_maximum_fusion.9
  168.8 0.7 dynamic_slice.19
  170.2 0.6 fusion.57
  171.5 0.6 slice_bitcast_fusion.10
  172.2 0.5 copy-done.1
  172.7 0.3 copy-done.2
  173.0 0.4 constant_dynamic-slice_fusion.3
  173.4 0.7 copy.87
  174.2 5.1 %conditional.6 = (f32[1,4,256]{2,1,0:T(4,128)}, f32[1,4,256]{2,1,0:T(4,128)S(1)}, f32[1,4,256,128]{3,2,1,0:T(8,128)S(1)}) conditional(s32[]{:T(128)} %convert_element_type.81, (f32[4,256]{1,0:T(4,128)}, f32[4,256]{1,0:T(4,128)S(1)}, f32[4,256,128]{2,1,0:T(8,128)S(1)}) %tuple.139, (s32[]{:T(128)}, s32[2,256]{1,0:T(2,128)S(1)}, ...), branch_computations={%region_8.8_spmd, %region_9.11_spmd} | conditional | flops 275646976 | bytes 9239580 | solution.py:146
  174.4 0.6 fusion.14
  175.0 0.6 max.5
  175.5 1.5 fusion.16
  177.0 0.7 add_bitcast_fusion.1
  177.7 1.6 fusion.17
  179.9 0.7 copy.93
  180.6 5.1 %conditional.7 = (f32[1,4,256]{2,1,0:T(4,128)}, f32[1,4,256]{2,1,0:T(4,128)S(1)}, f32[1,4,256,128]{3,2,1,0:T(8,128)S(1)}) conditional(s32[]{:T(128)} %convert_element_type.82, (f32[4,256]{1,0:T(4,128)}, f32[4,256]{1,0:T(4,128)S(1)}, f32[4,256,128]{2,1,0:T(8,128)S(1)}) %tuple.141, (s32[]{:T(128)}, s32[2,256]{1,0:T(2,128)S(1)}, ...), branch_computations={%region_4.4_spmd, %region_5.7_spmd} | conditional | flops 275646976 | bytes 9239580 | solution.py:146
  180.8 0.6 fusion.2
  181.4 0.6 max.4
  182.0 1.5 fusion.4
  183.4 0.7 add_bitcast_fusion
  184.1 1.6 fusion.5
  185.7 0.7 pad_maximum_fusion.9
  186.8 0.4 fusion.26
  187.4 0.4 fusion.27
  187.9 0.8 pad_maximum_fusion.3
  (83 shorter events, 3.2 us)
Async XLA Ops:
  7.2 1.2 copy-start
  7.2 8.9 %copy-start.9 = (u32[32]{0:T(128)S(1)}, u32[32]{0:T(128)}, u32[]{:S(2)}) copy-start(u32[32]{0:T(128)} %constant.92) | copy-start | bytes 388
  7.2 10.1 %copy-start.4 = (bf16[512,256]{1,0:T(8,128)(2,1)S(1)}, bf16[512,256]{1,0:T(8,128)(2,1)}, u32[]{:S(2)}) copy-start(bf16[512,256]{1,0:T(8,128)(2,1)} %param.15) | copy-start | bytes 786436
  7.2 3.7 %copy-start.8 = (s32[1,3]{1,0:T(1,128)S(1)}, s32[1,3]{1,0:T(1,128)}, u32[]{:S(2)}) copy-start(s32[1,3]{1,0:T(1,128)} %param.17) | copy-start | bytes 40
  7.2 61.5 %copy-start.6 = (bf16[64,512]{1,0:T(8,128)(2,1)S(1)}, bf16[64,512]{1,0:T(8,128)(2,1)}, u32[]{:S(2)}) copy-start(bf16[64,512]{1,0:T(8,128)(2,1)} %param.14) | copy-start | bytes 196612
  7.2 61.5 %copy-start.7 = (bf16[64,512]{1,0:T(8,128)(2,1)S(1)}, bf16[64,512]{1,0:T(8,128)(2,1)}, u32[]{:S(2)}) copy-start(bf16[64,512]{1,0:T(8,128)(2,1)} %param.13) | copy-start | bytes 196612
  7.2 63.0 %copy-start.5 = (bf16[64,4096]{1,0:T(8,128)(2,1)S(1)}, bf16[64,4096]{1,0:T(8,128)(2,1)}, u32[]{:S(2)}) copy-start(bf16[64,4096]{1,0:T(8,128)(2,1)} %param.12) | copy-start | bytes 1572868
  7.2 60.1 %reduce-scatter.2.cloned.1.call-start = ((), (), s32[]{:S(2)}) async-start(), calls=%async_computation.1 | async-start | bytes 1114112 | tf_op jit(solution)/shard_map/reduce_scatter | solution.py:83
  10.8 98.4 %all-gather.3.cloned.1.call-start = ((), (), s32[]{:S(2)}) async-start(), calls=%async_computation.2 | async-start | bytes 1114112 | tf_op jit(solution)/shard_map/all_gather | solution.py:132
  69.5 79.4 %all-gather.5.cloned.1.call-start = ((), (), s32[]{:S(2)}) async-start(), calls=%async_computation.3 | async-start | bytes 1114112 | tf_op jit(solution)/shard_map/all_gather | solution.py:133
  153.7 1.2 copy-start.1
  153.8 1.5 copy-start.2
  155.3 1.2 copy-start.3
  171.4 1.2 copy-start.1
  171.4 1.5 copy-start.2
  173.0 1.2 copy-start.3
Sparse Core Ops, SparseCore 0:
  11.7 55.6 reduce-scatter.1
  70.1 39.1 all-gather.2
  112.0 36.8 all-gather.4
where the time goes:
time: 196 us; the launch traced here: 195 us
  waiting for transfers between devices  97.6 us (50%)
  blocking collectives  25.9 us (13%)
  other arithmetic  19.3 us (10%)
  between operations  19.2 us (10%)
  local copies, waits for them, and re-layouts  17.6 us (9%)
  matrix products  11.3 us (6%)
  loops' own time  4.18 us (2%)
    all_gather x1, waiting for transfers between devices, body(): piece_keys = lax.all_gather(cache_keys, 'ctx', axis=0, tiled=True)  37.9 us
    all_gather x1, waiting for transfers between devices, body(): piece_values = lax.all_gather(cache_values, 'ctx', axis=0, tiled=True)  37.4 us
    unnamed x1, blocking collectives  25.9 us
    reduce_scatter x1, waiting for transfers between devices, body(): lax.psum_scatter(partial_kv, 'ctx', scatter_dimension=0, tiled=True)  21.6 us
    dot_general x4, matrix products, update(): jnp.einsum('grk,kgd->grd', weight.astype(jnp.bfloat16), block_values, pre...  6.43 us
    reduce_sum x4, other arithmetic, update(): running_sum = running_sum * shrink + jnp.sum(weight, axis=-1)  5.93 us
    while x16, local copies, waits for them, and re-layouts  4.29 us
    another operation x10, other arithmetic, scan_step(): jnp.stack([outcome[0][number_index], outcome[1][number_index]])  4.27 us
  transfers between devices with their start and end apart: 3, of which 3 were waited for; matrix products, arithmetic and copies ran while one was open for 4% of the time, Pallas kernels for 0%

commit v1 on v0

--- a/solution.py
+++ b/solution.py
@@ -129,7 +129,19 @@
         jnp.zeros((2, kv_count, query_span), jnp.float32),
         jnp.zeros((2, kv_count, query_span, HEAD_DIM), jnp.float32),
     )
-    piece_keys = lax.all_gather(cache_keys, "ctx", axis=0, tiled=True)
+    current_arr, known = (lax.axis_size("ctx"), lax.axis_index("ctx"))
+    piece_keys, z2 = (cache_keys, 1)
+    while z2 < current_arr:
+        pile = []
+        j0 = 0
+        while j0 < current_arr:
+            pile.append((j0, j0 ^ z2))
+            j0 += 1
+        current_block = lax.ppermute(piece_keys, "ctx", perm=pile)
+        v_next = jnp.concatenate([piece_keys, current_block], axis=0)
+        q_next = jnp.concatenate([current_block, piece_keys], axis=0)
+        piece_keys = jnp.where(known & z2 == 0, v_next, q_next)
+        z2 = 2 * z2
     piece_values = lax.all_gather(cache_values, "ctx", axis=0, tiled=True)
     piece_size = piece_keys.shape[0]
     block_size = math.gcd(piece_size, 512)

time: 196 us -> 171 us (0.87)
  waiting for transfers between devices: 97.6 us -> 65.4 us
  starting transfers between devices: 0.12 us -> 5.66 us
    all_gather x1 -> x0, waiting for transfers between devices: 37.9 us -> none  [body(): piece_keys = lax.all_gather(cache_keys, 'ctx', axis=0, tiled=True)]
    ppermute x0 -> x4, waiting for transfers between devices: none -> 36.5 us  [body(): current_block = lax.ppermute(piece_keys, 'ctx', perm=pile)]
    all_gather x1, waiting for transfers between devices: 37.4 us -> 7.25 us  [body(): piece_values = lax.all_gather(cache_values, 'ctx', axis=0, tiled=True)]
    ppermute x0 -> x4, starting transfers between devices: none -> 5.58 us  [body(): current_block = lax.ppermute(piece_keys, 'ctx', perm=pile)]
    reshape x1 -> x0, local copies, waits for them, and re-layouts: 2.16 us -> none  [body(): split_keys = piece_keys.reshape(block_count, block_size, kv_count, HEAD_DIM)]
  transfers between devices with their start and end apart: 3 -> 6, of which waited for: 3 -> 6; matrix products, arithmetic and copies ran while one was open for 4% -> 5% of each run, Pallas kernels for 0% -> 0%
where the time goes in v1:
time: 171 us; the launch traced here: 170 us
  waiting for transfers between devices  65.4 us (38%)
  blocking collectives  25.9 us (15%)
  other arithmetic  20.1 us (12%)
  between operations  19.5 us (11%)
  local copies, waits for them, and re-layouts  17.6 us (10%)
  matrix products  11.4 us (7%)
  starting transfers between devices  5.66 us (3%)
  loops' own time  4.21 us (2%)
    ppermute x4, waiting for transfers between devices, body(): current_block = lax.ppermute(piece_keys, 'ctx', perm=pile)  36.5 us
    unnamed x1, blocking collectives  25.9 us
    reduce_scatter x1, waiting for transfers between devices, body(): lax.psum_scatter(partial_kv, 'ctx', scatter_dimension=0, tiled=True)  21.6 us
    all_gather x1, waiting for transfers between devices, body(): piece_values = lax.all_gather(cache_values, 'ctx', axis=0, tiled=True)  7.25 us
    dot_general x4, matrix products, update(): jnp.einsum('grk,kgd->grd', weight.astype(jnp.bfloat16), block_values, pre...  6.52 us
    reduce_sum x4, other arithmetic, update(): running_sum = running_sum * shrink + jnp.sum(weight, axis=-1)  5.94 us
    ppermute x4, starting transfers between devices, body(): current_block = lax.ppermute(piece_keys, 'ctx', perm=pile)  5.58 us
    another operation x10, other arithmetic, scan_step(): jnp.stack([outcome[0][number_index], outcome[1][number_index]])  4.29 us
  transfers between devices with their start and end apart: 6, of which 6 were waited for; matrix products, arithmetic and copies ran while one was open for 5% of the time, Pallas kernels for 0%

profile of v1, /device:TPU:25, one launch (start us, length us, event | category | flops | bytes accessed | tf_op | source)
XLA Modules:
  0.0 169.7 jit_solution(17624262522089523670)
XLA Ops:
  7.3 1.1 copy-done
  8.4 2.4 %fusion.47 = f32[256,1024]{1,0:T(8,128)} fusion(bf16[512,256]{1,0:T(8,128)(2,1)} %param.15, bf16[512,1024]{1,0:T(8,128)(2,1)S(1)} %copy-done), kind=kOutput, calls=%fused_computation.108 | convolution fusion | flops 268435456 | bytes 2359296 | tf_op jit(solution)/shard_map/dot_general | solution.py:77
  10.9 0.6 fusion.46
  16.0 0.6 dynamic-slice
  17.4 25.9 %all-reduce = f32[256]{0:T(256)S(1)} all-reduce(f32[256]{0:T(256)S(1)} %multiply_reduce_fusion), channel_id=3, replica_groups=mesh['groups'=2,'ctx'=16] {'ctx'}, use_global_device_ids=true, to_apply=%region_2.0.clone | all-reduce | flops 256 | bytes 2048
  43.3 0.7 iota_add_fusion.2
  44.0 0.7 compare_and_fusion
  44.7 0.8 fusion.39
  45.8 21.6 %reduce-scatter.2.cloned.1.call-done = f32[16,1024]{1,0:T(8,128)} async-done(((f32[256,1024]{1,0:T(8,128)}), f32[16,1024]{1,0:T(8,128)}) %reduce-scatter.2.cloned.1.call-update) | async-done | bytes 65552 | tf_op jit(solution)/shard_map/reduce_scatter | solution.py:83
  67.4 0.9 broadcast_multiply_fusion
  68.7 0.7 slice_select_fusion
  69.4 2.7 %collective-permute-start = (bf16[64,512]{1,0:T(8,128)(2,1)S(1)}, bf16[64,512]{1,0:T(8,128)(2,1)S(1)}, u32[]{:S(2)}, u32[]{:S(2)}) collective-permute-start(bf16[64,512]{1,0:T(8,128)(2,1)S(1)} %get-tuple-element.298), channel_id=1, source_target_pairs={{0,1},{1,0},{2,3},{3,2},{4,5},{5,4},{6,7},{7,6},{8,9},{9,8},{10,11... | collective-permute-start | bytes 196616 | tf_op jit(solution)/shard_map/ppermute | solution.py:140
  72.1 0.9 collective-permute-done
  73.4 4.4 %collective-permute-done.1 = bf16[128,512]{1,0:T(8,128)(2,1)S(1)} collective-permute-done((bf16[128,512]{1,0:T(8,128)(2,1)S(1)}, bf16[128,512]{1,0:T(8,128)(2,1)S(1)}, u32[]{:S(2)}, u32[]{:S(2)}) %collective-permute-start.1) | collective-permute-done | bytes 131104 | tf_op jit(solution)/shard_map/ppermute | solution.py:140
  78.2 7.5 %collective-permute-done.2 = bf16[256,512]{1,0:T(8,128)(2,1)S(1)} collective-permute-done((bf16[256,512]{1,0:T(8,128)(2,1)S(1)}, bf16[256,512]{1,0:T(8,128)(2,1)S(1)}, u32[]{:S(2)}, u32[]{:S(2)}) %collective-permute-start.2) | collective-permute-done | bytes 262176 | tf_op jit(solution)/shard_map/ppermute | solution.py:140
  86.0 2.2 %collective-permute-start.3 = (bf16[512,512]{1,0:T(8,128)(2,1)S(1)}, bf16[512,512]{1,0:T(8,128)(2,1)S(1)}, u32[]{:S(2)}, u32[]{:S(2)}) collective-permute-start(bf16[512,512]{1,0:T(8,128)(2,1)S(1)} %maximum_select_fusion.1), channel_id=1, source_target_pairs={{0,8},{1,9},{2,10},{3,11},{4,12},{5,13},{6,14},{7,15},{8,0},{9,1},... | collective-permute-start | bytes 1572872 | tf_op jit(solution)/shard_map/ppermute | solution.py:140
  88.2 1.1 slice_bitcast_fusion.6
  89.5 0.8 copy.26
  90.3 23.7 %collective-permute-done.3 = bf16[512,512]{1,0:T(8,128)(2,1)S(1)} collective-permute-done((bf16[512,512]{1,0:T(8,128)(2,1)S(1)}, bf16[512,512]{1,0:T(8,128)(2,1)S(1)}, u32[]{:S(2)}, u32[]{:S(2)}) %collective-permute-start.3) | collective-permute-done | bytes 524320 | tf_op jit(solution)/shard_map/ppermute | solution.py:140
  114.0 0.5 maximum_select_fusion
  114.5 1.1 select_n.110
  115.6 7.3 %all-gather.2.cloned.1.call-done = bf16[1024,512]{1,0:T(8,128)(2,1)} async-done(((bf16[64,512]{1,0:T(8,128)(2,1)}), bf16[1024,512]{1,0:T(8,128)(2,1)}) %all-gather.2.cloned.1.call-update) | async-done | bytes 1048592 | tf_op jit(solution)/shard_map/all_gather | solution.py:145
  122.9 2.1 %reshape.195 = bf16[2,512,4,128]{3,2,1,0:T(4,128)(2,1)} reshape(bf16[1024,512]{1,0:T(8,128)(2,1)} %all-gather.2.cloned.1.call-done) | data formatting | bytes 2097152 | tf_op jit(solution)/shard_map/reshape | solution.py:150
  125.1 35.5 %while.15 = (s32[]{:T(128)}, f32[2,4,256]{2,1,0:T(4,128)S(1)}, f32[2,4,256]{2,1,0:T(4,128)S(1)}, f32[2,4,256,128]{3,2,1,0:T(8,128)S(1)}, s32[2]{0:T(128)S(1)}, /...) while((s32[]{:T(128)}, f32[2,4,256]{2,1,0:T(4,128)S(1)}, ...), condition=%wide.region_12.13_spmd.clone, body=%wide.region_3.12_spmd.clone.sunk | while | flops 551560704 | bytes 36390424 | solution.py:180
  125.1 0.6 dynamic_slice.19
  126.3 0.7 fusion.57
  127.7 0.6 slice_bitcast_fusion.10
  128.5 0.5 copy-done.1
  129.7 0.7 copy.87
  130.4 5.1 %conditional.6 = (f32[1,4,256]{2,1,0:T(4,128)}, f32[1,4,256]{2,1,0:T(4,128)S(1)}, f32[1,4,256,128]{3,2,1,0:T(8,128)S(1)}) conditional(s32[]{:T(128)} %convert_element_type.81, (f32[4,256]{1,0:T(4,128)}, f32[4,256]{1,0:T(4,128)S(1)}, f32[4,256,128]{2,1,0:T(8,128)S(1)}) %tuple.139, (s32[]{:T(128)}, s32[2,256]{1,0:T(2,128)S(1)}, ...), branch_computations={%region_8.8_spmd, %region_9.11_spmd} | conditional | flops 275646976 | bytes 9239580 | solution.py:158
  130.6 0.6 fusion.14
  131.2 0.6 max.5
  131.8 1.5 fusion.16
  133.3 0.7 add_bitcast_fusion.1
  134.0 1.6 fusion.17
  136.2 0.7 copy.93
  136.9 5.2 %conditional.7 = (f32[1,4,256]{2,1,0:T(4,128)}, f32[1,4,256]{2,1,0:T(4,128)S(1)}, f32[1,4,256,128]{3,2,1,0:T(8,128)S(1)}) conditional(s32[]{:T(128)} %convert_element_type.82, (f32[4,256]{1,0:T(4,128)}, f32[4,256]{1,0:T(4,128)S(1)}, f32[4,256,128]{2,1,0:T(8,128)S(1)}) %tuple.141, (s32[]{:T(128)}, s32[2,256]{1,0:T(2,128)S(1)}, ...), branch_computations={%region_4.4_spmd, %region_5.7_spmd} | conditional | flops 275646976 | bytes 9239580 | solution.py:158
  137.1 0.6 fusion.2
  137.6 0.6 max.4
  138.2 1.5 fusion.4
  139.7 0.7 add_bitcast_fusion
  140.4 1.6 fusion.5
  142.1 0.7 pad_maximum_fusion.9
  142.9 0.6 dynamic_slice.19
  144.1 0.7 fusion.57
  145.5 0.6 slice_bitcast_fusion.10
  146.2 0.5 copy-done.1
  147.5 0.7 copy.87
  148.2 5.1 %conditional.6 = (f32[1,4,256]{2,1,0:T(4,128)}, f32[1,4,256]{2,1,0:T(4,128)S(1)}, f32[1,4,256,128]{3,2,1,0:T(8,128)S(1)}) conditional(s32[]{:T(128)} %convert_element_type.81, (f32[4,256]{1,0:T(4,128)}, f32[4,256]{1,0:T(4,128)S(1)}, f32[4,256,128]{2,1,0:T(8,128)S(1)}) %tuple.139, (s32[]{:T(128)}, s32[2,256]{1,0:T(2,128)S(1)}, ...), branch_computations={%region_8.8_spmd, %region_9.11_spmd} | conditional | flops 275646976 | bytes 9239580 | solution.py:158
  148.4 0.6 fusion.14
  149.0 0.6 max.5
  149.6 1.5 fusion.16
  151.0 0.7 add_bitcast_fusion.1
  151.7 1.6 fusion.17
  154.0 0.7 copy.93
  154.7 5.2 %conditional.7 = (f32[1,4,256]{2,1,0:T(4,128)}, f32[1,4,256]{2,1,0:T(4,128)S(1)}, f32[1,4,256,128]{3,2,1,0:T(8,128)S(1)}) conditional(s32[]{:T(128)} %convert_element_type.82, (f32[4,256]{1,0:T(4,128)}, f32[4,256]{1,0:T(4,128)S(1)}, f32[4,256,128]{2,1,0:T(8,128)S(1)}) %tuple.141, (s32[]{:T(128)}, s32[2,256]{1,0:T(2,128)S(1)}, ...), branch_computations={%region_4.4_spmd, %region_5.7_spmd} | conditional | flops 275646976 | bytes 9239580 | solution.py:158
  154.8 0.6 fusion.2
  155.4 0.6 max.4
  156.0 1.5 fusion.4
  157.5 0.7 add_bitcast_fusion
  158.2 1.6 fusion.5
  159.9 0.7 pad_maximum_fusion.9
  160.9 0.4 fusion.26
  162.0 0.8 pad_maximum_fusion.3
  (92 shorter events, 6.0 us)
Async XLA Ops:
  7.2 1.2 copy-start
  7.2 8.9 %copy-start.9 = (u32[32]{0:T(128)S(1)}, u32[32]{0:T(128)}, u32[]{:S(2)}) copy-start(u32[32]{0:T(128)} %constant.99) | copy-start | bytes 388
  7.2 10.1 %copy-start.4 = (bf16[512,256]{1,0:T(8,128)(2,1)S(1)}, bf16[512,256]{1,0:T(8,128)(2,1)}, u32[]{:S(2)}) copy-start(bf16[512,256]{1,0:T(8,128)(2,1)} %param.15) | copy-start | bytes 786436
  7.2 3.7 %copy-start.8 = (s32[1,3]{1,0:T(1,128)S(1)}, s32[1,3]{1,0:T(1,128)}, u32[]{:S(2)}) copy-start(s32[1,3]{1,0:T(1,128)} %param.17) | copy-start | bytes 40
  7.2 61.5 %copy-start.6 = (bf16[64,512]{1,0:T(8,128)(2,1)S(1)}, bf16[64,512]{1,0:T(8,128)(2,1)}, u32[]{:S(2)}) copy-start(bf16[64,512]{1,0:T(8,128)(2,1)} %param.14) | copy-start | bytes 196612
  7.2 61.5 %copy-start.7 = (bf16[64,512]{1,0:T(8,128)(2,1)S(1)}, bf16[64,512]{1,0:T(8,128)(2,1)}, u32[]{:S(2)}) copy-start(bf16[64,512]{1,0:T(8,128)(2,1)} %param.13) | copy-start | bytes 196612
  7.2 60.1 %reduce-scatter.2.cloned.1.call-start = ((), (), s32[]{:S(2)}) async-start(), calls=%async_computation.1 | async-start | bytes 1114112 | tf_op jit(solution)/shard_map/reduce_scatter | solution.py:83
  10.8 112.0 %all-gather.2.cloned.1.call-start = ((), (), s32[]{:S(2)}) async-start(), calls=%async_computation.2 | async-start | bytes 1114112 | tf_op jit(solution)/shard_map/all_gather | solution.py:145
  69.4 20.0 %copy-start.5 = (bf16[64,512]{1,0:T(8,128)(2,1)}, bf16[64,512]{1,0:T(8,128)(2,1)S(1)}, u32[]{:S(2)}) copy-start(bf16[64,512]{1,0:T(8,128)(2,1)S(1)} %get-tuple-element.298) | copy-start | bytes 196612
  69.4 3.6 %collective-permute-start = (bf16[64,512]{1,0:T(8,128)(2,1)S(1)}, bf16[64,512]{1,0:T(8,128)(2,1)S(1)}, u32[]{:S(2)}, u32[]{:S(2)}) collective-permute-start(bf16[64,512]{1,0:T(8,128)(2,1)S(1)} %get-tuple-element.298), channel_id=1, source_target_pairs={{0,1},{1,0},{2,3},{3,2},{4,5},{5,4},{6,7},{7,6},{8,9},{9,8},{10,11... | collective-permute-start | bytes 196616 | tf_op jit(solution)/shard_map/ppermute | solution.py:140
  73.1 4.8 %collective-permute-start.1 = (bf16[128,512]{1,0:T(8,128)(2,1)S(1)}, bf16[128,512]{1,0:T(8,128)(2,1)S(1)}, u32[]{:S(2)}, u32[]{:S(2)}) collective-permute-start(bf16[128,512]{1,0:T(8,128)(2,1)S(1)} %maximum_select_fusion.3), channel_id=1, source_target_pairs={{0,2},{1,3},{2,0},{3,1},{4,6},{5,7},{6,4},{7,5},{8,10},{9,11},{10,... | collective-permute-start | bytes 393224 | tf_op jit(solution)/shard_map/ppermute | solution.py:140
  77.9 7.9 %collective-permute-start.2 = (bf16[256,512]{1,0:T(8,128)(2,1)S(1)}, bf16[256,512]{1,0:T(8,128)(2,1)S(1)}, u32[]{:S(2)}, u32[]{:S(2)}) collective-permute-start(bf16[256,512]{1,0:T(8,128)(2,1)S(1)} %maximum_select_fusion.2), channel_id=1, source_target_pairs={{0,4},{1,5},{2,6},{3,7},{4,0},{5,1},{6,2},{7,3},{8,12},{9,13},{10,... | collective-permute-start | bytes 786440 | tf_op jit(solution)/shard_map/ppermute | solution.py:140
  86.0 28.1 %collective-permute-start.3 = (bf16[512,512]{1,0:T(8,128)(2,1)S(1)}, bf16[512,512]{1,0:T(8,128)(2,1)S(1)}, u32[]{:S(2)}, u32[]{:S(2)}) collective-permute-start(bf16[512,512]{1,0:T(8,128)(2,1)S(1)} %maximum_select_fusion.1), channel_id=1, source_target_pairs={{0,8},{1,9},{2,10},{3,11},{4,12},{5,13},{6,14},{7,15},{8,0},{9,1},... | collective-permute-start | bytes 1572872 | tf_op jit(solution)/shard_map/ppermute | solution.py:140
  127.7 1.2 copy-start.1
  127.7 1.5 copy-start.2
  129.2 1.2 copy-start.3
  145.5 1.2 copy-start.1
  145.5 1.5 copy-start.2
  147.0 1.2 copy-start.3
Sparse Core Ops, SparseCore 0:
  11.7 55.6 reduce-scatter.1
  70.1 52.7 all-gather.1
